TPU v7x, 256 devices: a whole 4x4x8 slice. The times are simulated.
256 devices in a mesh: pipe: 2 (over core), dp: 128 (over x, y, z).
Axes of the slice: x: 4, y: 4, z: 8, core: 2. Of those that a mesh axis runs over, the one named last changes fastest.
Arguments:
- tokens: bfloat16 [4, 4096, 2048], P(None, 'dp'), may hold values from -40 to 40
- seg_ids: int32 [4, 4096], P(None, 'dp'), may hold values from 0 to 31, as said below
- cache_row: int32 [4, 4096], P(None, 'dp'), may hold values from 0 to 16383, as said below
- ln_gain: float32 [2, 2048], P('pipe'), may hold values from 0.1 to 1.9
- ln_bias: float32 [2, 2048], P('pipe'), may hold values from -2 to 2
- qkv_weight: bfloat16 [2, 2048, 3072], P('pipe', 'dp'), may hold values from -8 to 8
- qkv_bias: float32 [2, 3072], P('pipe'), may hold values from -3 to 3
- out_weight: bfloat16 [2, 1024, 2048], P('pipe', 'dp'), may hold values from -0.1875 to 0.1875
- out_bias: float32 [2, 2048], P('pipe'), may hold values from -2 to 2
Outputs:
- hidden: bfloat16 [2, 4, 4096, 2048], P('pipe', None, 'dp')
- kv_cache: bfloat16 [2, 16384, 2048], P('pipe', 'dp')
Inputs may be any that keep to these rules, and one draw needn't show every extreme that they name: `seg_ids`: each block of 32 tokens of a micro-batch holds whole prompts, numbered from 0 in order, never crossing the block's edges. In every micro-batch one block holds a single prompt of 32 tokens and another holds 32 prompts of one token. `cache_row`: over all micro-batches each cache row is named once. Rows d * 4 * 32 to (d + 1) * 4 * 32 - 1 belong to index d of dp, which gets 32 of them in each micro-batch. Of the 32 tokens of one index of dp in one micro-batch, each owner gets none or exactly 2.
All inputs are finite; a program needn't handle non-finite values.
Results may differ from a plain program's by a relative error of at most 0.0065.
Values may be sent and summed in bfloat16 or wider, within the bound.
No kernel may reach another device: no remote copies, remote signals or barrier semaphores. Data moves between devices by JAX's collectives and lax.ppermute only.
A program may use at most 128 MiB of HBM per device.

v0:
```python
import jax
import jax.numpy as jnp
from jax import lax
from jax.sharding import PartitionSpec as P

HEADS = 4
HDIM = 256
ROT = 64
HALF = ROT // 2
EPS = 1e-05
META = 128
BF = jnp.bfloat16
F32 = jnp.float32


def swap(value):
    return lax.ppermute(value, "pipe", [(0, 1), (1, 0)])


def mm(a, b):
    return jnp.dot(a, b, preferred_element_type=F32)


def layer_norm(layer_in, gain_row, shift_row):
    data = layer_in.astype(F32)
    centre = jnp.mean(data, axis=-1, keepdims=True)
    centred = data - centre
    variance = jnp.mean(centred * centred, axis=-1, keepdims=True)
    return (centred * lax.rsqrt(variance + EPS) * gain_row + shift_row).astype(BF)


def angles_of(positions):
    inverse = 10000.0 ** (-2.0 * jnp.arange(HALF, dtype=F32) / ROT)
    angles = positions[:, None] * inverse[None, :]
    return (jnp.cos(angles), jnp.sin(angles))


def rotary(head_cols, cos_sin):
    cosine, sine = cos_sin
    out = []
    for first in range(0, head_cols.shape[1], HDIM):
        leading = head_cols[:, first : first + HALF]
        trailing = head_cols[:, first + HALF : first + ROT]
        out += [
            leading * cosine - trailing * sine,
            trailing * cosine + leading * sine,
            head_cols[:, first + ROT : first + HDIM],
        ]
    return jnp.concatenate(out, axis=-1)


def attend(queries, key_rows, value_rows, allowed):
    parts = []
    for first in range(0, queries.shape[1], HDIM):
        one = slice(first, first + HDIM)
        scores = lax.dot_general(
            queries[:, one], key_rows[:, one], (((1,), (1,)), ((), ())), preferred_element_type=F32
        ) * HDIM ** (-0.5)
        scores = jnp.where(allowed, scores, -1e30)
        exp_scores = jnp.exp(scores - jnp.max(scores, axis=-1, keepdims=True))
        probs = (exp_scores / jnp.sum(exp_scores, axis=-1, keepdims=True)).astype(BF)
        parts.append(mm(probs, value_rows[:, one]).astype(BF))
    return jnp.concatenate(parts, axis=-1)


def shards(
    tokens, seg_ids, cache_row, ln_gain, ln_bias, qkv_weight, qkv_bias, out_weight, out_bias
):
    micro_count, row_count, width = tokens.shape
    device_count = lax.axis_size("dp")
    core = lax.axis_index("pipe")
    first_core = core == 0
    cache_size = micro_count * row_count
    slot_cap = 2 * micro_count * ((row_count + device_count - 1) // device_count)
    head_width = qkv_weight.shape[2] // 3
    half_heads = head_width // 2
    half_width = width // 2

    def pick(a, b):
        return jnp.where(first_core, a, b)

    qkv_shard = qkv_weight[0].reshape(-1, 3, 2, half_heads)
    out_shard = out_weight[0]

    def packed(which):
        qkv_part = qkv_shard[:, :, which, :].reshape(-1, 3 * half_heads)
        out_part = out_shard[:, which * half_width : (which + 1) * half_width]
        out_part = jnp.concatenate(
            [out_part[:, : half_width // 2], out_part[:, half_width // 2 :]], axis=0
        )
        return jnp.concatenate([qkv_part, out_part], axis=1)

    low, high = (packed(0), packed(1))
    kept = pick(low, high)
    got = swap(pick(high, low))
    both = jnp.concatenate([pick(kept, got), pick(got, kept)], axis=1)
    gathered = lax.all_gather(both, "dp", axis=0, tiled=True)
    vectors = jnp.concatenate([ln_gain[0], ln_bias[0], qkv_bias[0], out_bias[0]])
    vectors_got = swap(vectors)
    vectors_of = (pick(vectors, vectors_got), pick(vectors_got, vectors))

    def weights_of(layer):
        begin = layer * 2 * head_width
        qkv = gathered[:, begin : begin + 3 * half_heads]
        out = gathered[:, begin + 3 * half_heads : begin + 2 * head_width]
        out = out.reshape(device_count, 2, -1, half_heads)
        out = jnp.concatenate(
            [out[:, 0].reshape(head_width, half_heads), out[:, 1].reshape(head_width, half_heads)],
            axis=1,
        )
        other = swap(out)
        out = jnp.concatenate([pick(out, other), pick(other, out)], axis=1)
        vec = vectors_of[layer]
        gain = vec[:width]
        shift = vec[width : 2 * width]
        bias = vec[2 * width : 2 * width + 3 * head_width].reshape(3, 2, half_heads)
        bias = pick(bias[:, 0], bias[:, 1]).reshape(-1)
        out_b = vec[2 * width + 3 * head_width :]
        return (qkv, bias, out, out_b, gain, shift)

    flat = tokens.reshape(cache_size, width)
    seg = seg_ids.reshape(cache_size)
    rows = cache_row.reshape(cache_size)
    order = jnp.arange(cache_size, dtype=jnp.int32)
    micro = order // row_count
    same_micro = micro[:, None] == micro[None, :]
    positions = order % row_count - jnp.sum(
        (same_micro & (seg[None, :] < seg[:, None])).astype(jnp.int32), axis=1
    )
    earlier = order[None, :] <= order[:, None]
    allowed = same_micro & earlier & (seg[:, None] == seg[None, :])
    owners = rows // cache_size
    rank = (
        jnp.sum(
            (same_micro & earlier & (owners[:, None] == owners[None, :])).astype(jnp.int32), axis=1
        )
        - 1
    )
    slot = owners * slot_cap + micro * (slot_cap // micro_count) + rank
    slots = device_count * slot_cap
    send = (jnp.arange(slots, dtype=jnp.int32)[:, None] == slot[None, :]).astype(BF)

    def exchange(payload):
        cols = payload.shape[1]
        filled = mm(send, payload).astype(BF).reshape(device_count, slot_cap, cols)
        arrived = lax.all_to_all(filled, "dp", split_axis=0, concat_axis=0, tiled=True)
        return arrived.reshape(slots, cols)

    lane = jnp.arange(META, dtype=jnp.int32)[None, :]
    meta = jnp.where(
        lane == 0, (rows % cache_size + 1)[:, None], jnp.where(lane == 1, positions[:, None], 0)
    ).astype(BF)
    half_tokens = pick(flat[:, :half_width], flat[:, half_width:])
    arrived = exchange(jnp.concatenate([half_tokens, meta], axis=1))
    place = arrived[:, half_width].astype(jnp.int32) - 1
    take = (order[:, None] == place[None, :]).astype(BF)
    own = mm(take, arrived).astype(BF)
    own_half = own[:, :half_width]
    own_other = swap(own_half)
    own_tokens = jnp.concatenate([pick(own_half, own_other), pick(own_other, own_half)], axis=1)
    turn = angles_of(positions.astype(F32))
    own_turn = angles_of(own[:, half_width + 1].astype(F32))

    def keys_values(layer_in, weights, cos_sin):
        qkv, bias, _, _, gain, shift = weights
        normed = layer_norm(layer_in, gain, shift)
        projected = mm(normed, qkv[:, half_heads:]) + bias[half_heads:]
        return jnp.concatenate(
            [rotary(projected[:, :half_heads], cos_sin), projected[:, half_heads:]], axis=1
        ).astype(BF)

    def context_of(layer_in, weights):
        qkv, bias, _, _, gain, shift = weights
        normed = layer_norm(layer_in, gain, shift)
        projected = mm(normed, qkv) + bias
        queries = rotary(projected[:, :half_heads], turn).astype(BF)
        key_rows = rotary(projected[:, half_heads : 2 * half_heads], turn).astype(BF)
        return attend(queries, key_rows, projected[:, 2 * half_heads :].astype(BF), allowed)

    def finish(layer_in, context_half, weights):
        other = swap(context_half)
        context = jnp.concatenate([pick(context_half, other), pick(other, context_half)], axis=1)
        return (layer_in.astype(F32) + mm(context, weights[2]) + weights[3]).astype(BF)

    layer0, layer1 = (weights_of(0), weights_of(1))
    context0 = context_of(flat, layer0)
    own_context0 = mm(take, exchange(context0)).astype(BF)
    hidden0 = finish(flat, context0, layer0)
    own_kv0 = keys_values(own_tokens, layer0, own_turn)
    context1 = context_of(hidden0, layer1)
    hidden1 = finish(hidden0, context1, layer1)
    own_hidden0 = finish(own_tokens, own_context0, layer0)
    own_kv1 = keys_values(own_hidden0, layer1, own_turn)
    kept_kv = pick(own_kv0, own_kv1)
    got_kv = swap(pick(own_kv1, own_kv0))
    low_kv, high_kv = (pick(kept_kv, got_kv), pick(got_kv, kept_kv))
    cache = jnp.concatenate(
        [
            low_kv[:, :half_heads],
            high_kv[:, :half_heads],
            low_kv[:, half_heads:],
            high_kv[:, half_heads:],
        ],
        axis=1,
    )
    hidden = pick(hidden0, hidden1).reshape(1, micro_count, row_count, width)
    return (hidden, cache[None])


def solution(mesh):
    placed = (
        P(None, "dp", None),
        P(None, "dp"),
        P(None, "dp"),
        P("pipe", None),
        P("pipe", None),
        P("pipe", "dp", None),
        P("pipe", None),
        P("pipe", "dp", None),
        P("pipe", None),
    )
    return jax.shard_map(
        shards,
        mesh=mesh,
        in_specs=placed,
        out_specs=(P("pipe", None, "dp", None), P("pipe", "dp", None)),
        check_vma=False,
    )
```

profile of v0, /device:TPU:1, one launch (start us, length us, event | category | flops | bytes accessed | tf_op | source)
XLA Modules:
  0.0 268.0 jit_solution(13999180450505885761)
XLA Ops:
  9.5 3.3 %collective-permute-start.1 = (bf16[16,2048]{1,0:T(8,128)(2,1)S(1)}, bf16[16,2048]{1,0:T(8,128)(2,1)S(1)}, u32[]{:S(2)}, u32[]{:S(2)}) collective-permute-start(bf16[16,2048]{1,0:T(8,128)(2,1)S(1)} %broadcast_select_fusion.18), channel_id=1, source_target_pairs={{0,128},{128,0},{1,129},{129,1},{2,130},{130,2},{3,131},{131,3},{4... | collective-permute-start | bytes 196616 | tf_op jit(solution)/shard_map/ppermute | solution.py:17
  17.9 2.2 fusion.12
  20.1 13.8 %all-to-all-start = ((bf16[128,8,1152]{2,1,0:T(8,128)(2,1)}), bf16[128,8,1152]{2,1,0:T(8,128)(2,1)S(1)}, u32[]{:S(2)}, u32[]{:S(2)}) async-start(bf16[128,8,1152]{2,1,0:T(8,128)(2,1)} %fusion.12), calls=%async_computation | async-start | bytes 4718592 | tf_op jit(solution)/shard_map/all_to_all | solution.py:146
  36.2 66.5 %all-to-all-done = bf16[128,8,1152]{2,1,0:T(8,128)(2,1)S(1)} async-done(((bf16[128,8,1152]{2,1,0:T(8,128)(2,1)}), bf16[128,8,1152]{2,1,0:T(8,128)(2,1)S(1)}, u32[]{:S(2)}, u32[]{:S(2)}) %all-to-all-start) | async-done | bytes 2359328 | tf_op jit(solution)/shard_map/all_to_all | solution.py:146
  104.0 3.3 %collective-permute-start.6 = (bf16[128,1024]{0,1:T(8,128)(2,1)S(1)}, bf16[128,1024]{0,1:T(8,128)(2,1)S(1)}, u32[]{:S(2)}, u32[]{:S(2)}) collective-permute-start(bf16[128,1024]{0,1:T(8,128)(2,1)S(1)} %slice.489), channel_id=1, source_target_pairs={{0,128},{128,0},{1,129},{129,1},{2,130},{130,2},{3,131},{131,3},{4... | collective-permute-start | bytes 786440 | tf_op jit(solution)/shard_map/ppermute | solution.py:17
  109.7 69.0 %all-gather.2.cloned.1.call-done = bf16[2048,4096]{1,0:T(8,128)(2,1)} async-done(((bf16[16,4096]{1,0:T(8,128)(2,1)}), bf16[2048,4096]{1,0:T(8,128)(2,1)}) %all-gather.2.cloned.1.call-update) | async-done | bytes 16777232 | tf_op jit(solution)/shard_map/all_gather | solution.py:97
  178.7 5.6 %fusion.281 = (bf16[128,1536]{0,1:T(8,128)(2,1)S(1)}, f32[128,1536]{0,1:T(8,128)S(1)}) fusion(f32[1536]{0:T(1024)S(1)} %select_n.239, bf16[2048,4096]{1,0:T(8,128)(2,1)} %all-gather.2.cloned.1.call-done, bf16[128,2048]{0,1:T(8,128)(2,1)} %copy-done.5, f32[2048]{0:T(1024)S(1)} %get-tuple-element.73, f32[2048]{0:T(1024)S(1)} %get-tuple-element.71, ...), kind=kOutput, calls=%fused_computation.381 | convolution fusion | flops 807272448 | bytes 8018944 | tf_op jit(solution)/shard_map/dot_general | solution.py:21
  185.5 1.4 fusion.40
  186.9 10.2 %all-to-all-start.1 = ((bf16[128,8,512]{2,1,0:T(8,128)(2,1)}), bf16[128,8,512]{2,1,0:T(8,128)(2,1)}, u32[]{:S(2)}, u32[]{:S(2)}) async-start(bf16[128,8,512]{2,1,0:T(8,128)(2,1)} %fusion.40), calls=%async_computation.1 | async-start | bytes 2097152 | tf_op jit(solution)/shard_map/all_to_all | solution.py:146
  197.1 2.5 fusion.273
  199.8 1.7 pad_maximum_fusion.17
  201.5 1.4 collective-permute-start.3
  203.7 1.7 pad_maximum_fusion.18
  205.9 5.1 %fusion.288 = (bf16[128,1024]{0,1:T(8,128)(2,1)}, f32[128,1024]{0,1:T(8,128)}) fusion(f32[1024]{0:T(1024)S(1)} %bitcast.61, bf16[2048,4096]{1,0:T(8,128)(2,1)} %all-gather.2.cloned.1.call-done, f32[128]{0:T(128)S(1)} %add_rsqrt_fusion.2, f32[128]{0:T(128)S(1)} %broadcast_multiply_fusion.2, f32[2048]{0:T(1024)S(1)} %copy-done.21, f32[2048]{0:T(1024)S(1)} %copy-done.19, ...), kind=kOutput, calls=%fused_computation.388 | convolution fusion | flops 539492352 | bytes 5526528 | tf_op jit(solution)/shard_map/dot_general | solution.py:21
  211.7 14.6 %all-to-all-done.1 = bf16[128,8,512]{2,1,0:T(8,128)(2,1)} async-done(((bf16[128,8,512]{2,1,0:T(8,128)(2,1)}), bf16[128,8,512]{2,1,0:T(8,128)(2,1)}, u32[]{:S(2)}, u32[]{:S(2)}) %all-to-all-start.1) | async-done | bytes 1048608 | tf_op jit(solution)/shard_map/all_to_all | solution.py:146
  226.3 1.5 convolution_convert_fusion.3
  227.9 3.6 %collective-permute-start.7 = (bf16[128,512]{1,0:T(8,128)(2,1)S(1)}, bf16[128,512]{1,0:T(8,128)(2,1)S(1)}, u32[]{:S(2)}, u32[]{:S(2)}) collective-permute-start(bf16[128,512]{1,0:T(8,128)(2,1)S(1)} %convolution_convert_fusion.3), channel_id=1, source_target_pairs={{0,128},{128,0},{1,129},{129,1},{2,130},{130,2},{3,131},{131,3},{4... | collective-permute-start | bytes 393224 | tf_op jit(solution)/shard_map/ppermute | solution.py:17
  231.5 3.0 %broadcast_select_fusion.3 = (bf16[1024,1024]{1,0:T(8,128)(2,1)S(1)}, bf16[1024,1024]{1,0:T(8,128)(2,1)S(1)}) fusion(bf16[1024,1024]{1,0:T(8,128)(2,1)} %collective-permute-done.3, pred[]{:T(512)S(6)} %eq.103, bf16[1024,512]{1,0:T(8,128)(2,1)} %copy-done, bf16[1024,512]{1,0:T(8,128)(2,1)S(1)} %get-tuple-element.24), kind=kLoop, calls=%fused_computation.36 | loop fusion | flops 6291456 | bytes 8388609 | tf_op jit(solution)/shard_map/jit(_where)/select_n | solution.py:80
  234.5 1.8 convert_reduce_fusion.1
  236.6 5.6 %fusion.284 = (bf16[128,1536]{0,1:T(8,128)(2,1)S(1)}, f32[128,1536]{0,1:T(8,128)S(1)}) fusion(f32[1536]{0:T(1024)S(1)} %select_n.250, bf16[2048,4096]{1,0:T(8,128)(2,1)} %all-gather.2.cloned.1.call-done, bf16[128,2048]{0,1:T(8,128)(2,1)S(1)} %get-tuple-element.95, f32[2048]{0:T(1024)S(1)} %copy-done.17, f32[2048]{0:T(1024)S(1)} %copy-done.16, ...), kind=kOutput, calls=%fused_computation.384 | convolution fusion | flops 807272448 | bytes 8018944 | tf_op jit(solution)/shard_map/dot_general | solution.py:21
  243.8 2.6 broadcast_select_fusion.1
  246.5 1.8 fusion.287
  248.6 4.2 %fusion.289 = (bf16[128,1024]{0,1:T(8,128)(2,1)S(1)}, f32[128,1024]{0,1:T(8,128)S(1)}) fusion(f32[1024]{0:T(1024)S(1)} %bitcast.60, bf16[2048,4096]{1,0:T(8,128)(2,1)} %all-gather.2.cloned.1.call-done, f32[128,2048]{0,1:T(8,128)S(1)} %get-tuple-element.103, f32[128]{0:T(128)S(1)} %add_rsqrt_fusion.1, f32[128]{0:T(128)S(1)} %broadcast_multiply_fusion.1, ...), kind=kOutput, calls=%fused_computation.389 | convolution fusion | flops 538443776 | bytes 6050816 | tf_op jit(solution)/shard_map/dot_general | solution.py:21
  257.2 1.8 fusion.37
  (169 shorter events, 25.2 us)
Async XLA Ops:
  7.2 171.5 %all-gather.2.cloned.1.call-start = ((), (), s32[]{:S(2)}) async-start(), calls=%async_computation.2 | async-start | bytes 16908288 | tf_op jit(solution)/shard_map/all_gather | solution.py:97
  9.5 4.2 %collective-permute-start.1 = (bf16[16,2048]{1,0:T(8,128)(2,1)S(1)}, bf16[16,2048]{1,0:T(8,128)(2,1)S(1)}, u32[]{:S(2)}, u32[]{:S(2)}) collective-permute-start(bf16[16,2048]{1,0:T(8,128)(2,1)S(1)} %broadcast_select_fusion.18), channel_id=1, source_target_pairs={{0,128},{128,0},{1,129},{129,1},{2,130},{130,2},{3,131},{131,3},{4... | collective-permute-start | bytes 196616 | tf_op jit(solution)/shard_map/ppermute | solution.py:17
  15.7 18.1 %copy-start.10 = (f32[1,3072]{1,0:T(1,128)S(1)}, f32[1,3072]{1,0:T(1,128)}, u32[]{:S(2)}) copy-start(f32[1,3072]{1,0:T(1,128)} %param.15) | copy-start | bytes 36868
  15.8 18.1 %copy-start.11 = (f32[1,2048]{1,0:T(1,128)S(1)}, f32[1,2048]{1,0:T(1,128)}, u32[]{:S(2)}) copy-start(f32[1,2048]{1,0:T(1,128)} %param.17) | copy-start | bytes 24580
  15.8 18.1 %copy-start.12 = (f32[1,2048]{1,0:T(1,128)S(1)}, f32[1,2048]{1,0:T(1,128)}, u32[]{:S(2)}) copy-start(f32[1,2048]{1,0:T(1,128)} %param.13) | copy-start | bytes 24580
  15.8 18.1 %copy-start.13 = (f32[1,2048]{1,0:T(1,128)S(1)}, f32[1,2048]{1,0:T(1,128)}, u32[]{:S(2)}) copy-start(f32[1,2048]{1,0:T(1,128)} %param.12) | copy-start | bytes 24580
  15.8 18.9 %copy-start.1 = (bf16[4,32,2048]{2,1,0:T(8,128)(2,1)S(1)}, bf16[4,32,2048]{2,1,0:T(8,128)(2,1)}, u32[]{:S(2)}) copy-start(bf16[4,32,2048]{2,1,0:T(8,128)(2,1)} %param.9) | copy-start | bytes 1572868
  17.5 167.5 %copy-start.23 = (s32[128]{0:T(128)}, s32[128]{0:T(128)S(1)}, u32[]{:S(2)}) copy-start(s32[128]{0:T(128)S(1)} %eq.107) | copy-start | bytes 1540
  17.6 167.5 %copy-start.25 = (s32[128]{0:T(128)}, s32[128]{0:T(128)S(1)}, u32[]{:S(2)}) copy-start(s32[128]{0:T(128)S(1)} %get-tuple-element.110) | copy-start | bytes 1540
  17.7 166.6 %copy-start.29 = (f32[128]{0:T(128)}, f32[128]{0:T(128)S(1)}, u32[]{:S(2)}) copy-start(f32[128]{0:T(128)S(1)} %get-tuple-element.12) | copy-start | bytes 1540
  20.1 82.6 %all-to-all-start = ((bf16[128,8,1152]{2,1,0:T(8,128)(2,1)}), bf16[128,8,1152]{2,1,0:T(8,128)(2,1)S(1)}, u32[]{:S(2)}, u32[]{:S(2)}) async-start(bf16[128,8,1152]{2,1,0:T(8,128)(2,1)} %fusion.12), calls=%async_computation | async-start | bytes 4718592 | tf_op jit(solution)/shard_map/all_to_all | solution.py:146
  33.9 1.6 collective-permute-start
  36.2 148.1 %copy-start.18 = (f32[2048]{0:T(1024)}, f32[2048]{0:T(1024)S(1)}, u32[]{:S(2)}) copy-start(f32[2048]{0:T(1024)S(1)} %get-tuple-element.71) | copy-start | bytes 24580
  36.2 148.1 %copy-start.20 = (f32[2048]{0:T(1024)}, f32[2048]{0:T(1024)S(1)}, u32[]{:S(2)}) copy-start(f32[2048]{0:T(1024)S(1)} %get-tuple-element.73) | copy-start | bytes 24580
  104.0 5.6 %collective-permute-start.6 = (bf16[128,1024]{0,1:T(8,128)(2,1)S(1)}, bf16[128,1024]{0,1:T(8,128)(2,1)S(1)}, u32[]{:S(2)}, u32[]{:S(2)}) collective-permute-start(bf16[128,1024]{0,1:T(8,128)(2,1)S(1)} %slice.489), channel_id=1, source_target_pairs={{0,128},{128,0},{1,129},{129,1},{2,130},{130,2},{3,131},{131,3},{4... | collective-permute-start | bytes 786440 | tf_op jit(solution)/shard_map/ppermute | solution.py:17
  109.7 93.4 %copy-start.2 = (bf16[128,1024]{0,1:T(8,128)(2,1)}, bf16[128,1024]{0,1:T(8,128)(2,1)S(1)}, u32[]{:S(2)}) copy-start(bf16[128,1024]{0,1:T(8,128)(2,1)S(1)} %get-tuple-element.45) | copy-start | bytes 786436
  186.9 39.3 %all-to-all-start.1 = ((bf16[128,8,512]{2,1,0:T(8,128)(2,1)}), bf16[128,8,512]{2,1,0:T(8,128)(2,1)}, u32[]{:S(2)}, u32[]{:S(2)}) async-start(bf16[128,8,512]{2,1,0:T(8,128)(2,1)} %fusion.40), calls=%async_computation.1 | async-start | bytes 2097152 | tf_op jit(solution)/shard_map/all_to_all | solution.py:146
  201.5 30.0 %collective-permute-start.3 = (bf16[1024,1024]{1,0:T(8,128)(2,1)}, bf16[1024,1024]{1,0:T(8,128)(2,1)}, u32[]{:S(2)}, u32[]{:S(2)}) collective-permute-start(bf16[1024,1024]{1,0:T(8,128)(2,1)} %pad_maximum_fusion.17), channel_id=1, source_target_pairs={{0,128},{128,0},{1,129},{129,1},{2,130},{130,2},{3,131},{131,3},{4... | collective-permute-start | bytes 6291464 | tf_op jit(solution)/shard_map/ppermute | solution.py:17
  203.4 7.5 %collective-permute-start.2 = (bf16[128,512]{1,0:T(8,128)(2,1)S(1)}, bf16[128,512]{1,0:T(8,128)(2,1)S(1)}, u32[]{:S(2)}, u32[]{:S(2)}) collective-permute-start(bf16[128,512]{1,0:T(8,128)(2,1)S(1)} %pad_maximum_fusion.21), channel_id=1, source_target_pairs={{0,128},{128,0},{1,129},{129,1},{2,130},{130,2},{3,131},{131,3},{4... | collective-permute-start | bytes 393224 | tf_op jit(solution)/shard_map/ppermute | solution.py:17
  205.4 38.4 %collective-permute-start.5 = (bf16[1024,1024]{1,0:T(8,128)(2,1)}, bf16[1024,1024]{1,0:T(8,128)(2,1)}, u32[]{:S(2)}, u32[]{:S(2)}) collective-permute-start(bf16[1024,1024]{1,0:T(8,128)(2,1)} %pad_maximum_fusion.18), channel_id=1, source_target_pairs={{0,128},{128,0},{1,129},{129,1},{2,130},{130,2},{3,131},{131,3},{4... | collective-permute-start | bytes 6291464 | tf_op jit(solution)/shard_map/ppermute | solution.py:17
  227.9 18.6 %collective-permute-start.7 = (bf16[128,512]{1,0:T(8,128)(2,1)S(1)}, bf16[128,512]{1,0:T(8,128)(2,1)S(1)}, u32[]{:S(2)}, u32[]{:S(2)}) collective-permute-start(bf16[128,512]{1,0:T(8,128)(2,1)S(1)} %convolution_convert_fusion.3), channel_id=1, source_target_pairs={{0,128},{128,0},{1,129},{129,1},{2,130},{130,2},{3,131},{131,3},{4... | collective-permute-start | bytes 393224 | tf_op jit(solution)/shard_map/ppermute | solution.py:17
  243.4 13.7 %collective-permute-start.4 = (bf16[128,512]{1,0:T(8,128)(2,1)S(1)}, bf16[128,512]{1,0:T(8,128)(2,1)S(1)}, u32[]{:S(2)}, u32[]{:S(2)}) collective-permute-start(bf16[128,512]{1,0:T(8,128)(2,1)S(1)} %pad_maximum_fusion.22), channel_id=1, source_target_pairs={{0,128},{128,0},{1,129},{129,1},{2,130},{130,2},{3,131},{131,3},{4... | collective-permute-start | bytes 393224 | tf_op jit(solution)/shard_map/ppermute | solution.py:17
  248.6 8.6 %copy-start.14 = (f32[2048]{0:T(1024)S(1)}, f32[2048]{0:T(1024)}, u32[]{:S(2)}) copy-start(f32[2048]{0:T(1024)} %get-tuple-element.69) | copy-start | bytes 24580
  256.5 3.4 %collective-permute-start.8 = (bf16[128,1024]{0,1:T(8,128)(2,1)S(1)}, bf16[128,1024]{0,1:T(8,128)(2,1)S(1)}, u32[]{:S(2)}, u32[]{:S(2)}) collective-permute-start(bf16[128,1024]{0,1:T(8,128)(2,1)S(1)} %broadcast_select_fusion.6), channel_id=1, source_target_pairs={{0,128},{128,0},{1,129},{129,1},{2,130},{130,2},{3,131},{131,3},{4... | collective-permute-start | bytes 786440 | tf_op jit(solution)/shard_map/ppermute | solution.py:17
  (19 other events, 81.5 us)
Sparse Core Ops, SparseCore 0:
  14.5 164.1 all-gather.1
where the time goes:
time: 269 us; the launch traced here: 268 us
  waiting for transfers between devices  151 us (56%)
  starting transfers between devices  37.8 us (14%)
  matrix products  33.7 us (13%)
  other arithmetic  17.5 us (7%)
  between operations  14.8 us (6%)
  local copies, waits for them, and re-layouts  12.9 us (5%)
    all_to_all x2, waiting for transfers between devices, exchange(): lax.all_to_all(filled, 'dp', split_axis=0, concat_axis=0, tiled=True)  81.1 us
    all_gather x1, waiting for transfers between devices, shards(): gathered = lax.all_gather(both, 'dp', axis=0, tiled=True)  69 us
    dot_general x15, matrix products, mm(): return jnp.dot(a, b, preferred_element_type=F32)  32.7 us
    all_to_all x2, starting transfers between devices, exchange(): lax.all_to_all(filled, 'dp', split_axis=0, concat_axis=0, tiled=True)  23.9 us
    ppermute x9, starting transfers between devices, swap(): return lax.ppermute(value, 'pipe', [(0, 1), (1, 0)])  13.8 us
    select_n x13, other arithmetic, pick(): return jnp.where(first_core, a, b)  6.67 us
  transfers between devices with their start and end apart: 12, of which 5 were waited for; matrix products, arithmetic and copies ran while one was open for 19% of the time, Pallas kernels for 0%

commit v1 on v0

--- a/solution.py
+++ b/solution.py
@@ -94,7 +94,9 @@
     kept = pick(low, high)
     got = swap(pick(high, low))
     both = jnp.concatenate([pick(kept, got), pick(got, kept)], axis=1)
-    gathered = lax.all_gather(both, "dp", axis=0, tiled=True)
+    gathered = jnp.concatenate(
+        lax.all_to_all(jnp.stack([both] * lax.axis_size("dp")), "dp", 0, 0), axis=0
+    )
     vectors = jnp.concatenate([ln_gain[0], ln_bias[0], qkv_bias[0], out_bias[0]])
     vectors_got = swap(vectors)
     vectors_of = (pick(vectors, vectors_got), pick(vectors_got, vectors))

time: 269 us -> 551 us (2.05); the launches traced: 268 us -> 543 us
  waiting for transfers between devices: 151 us -> 422 us
  between operations: 14.8 us -> 1.74 us
  starting transfers between devices: 37.8 us -> 49.7 us
  local copies, waits for them, and re-layouts: 12.9 us -> 18.6 us
    all_to_all x0 -> x1, waiting for transfers between devices: none -> 354 us  [shards(): lax.all_to_all(jnp.stack([both] * lax.axis_size('dp')), 'dp', 0, 0)]
    all_gather x1 -> x0, waiting for transfers between devices: 69 us -> none  [shards(): gathered = lax.all_gather(both, 'dp', axis=0, tiled=True)]
    all_to_all x2, waiting for transfers between devices: 81.1 us -> 66.4 us  [exchange(): lax.all_to_all(filled, 'dp', split_axis=0, concat_axis=0, tiled=True)]
    all_to_all x0 -> x1, starting transfers between devices: none -> 7.73 us  [shards(): lax.all_to_all(jnp.stack([both] * lax.axis_size('dp')), 'dp', 0, 0)]
    another operation x0 -> x1, local copies, waits for them, and re-layouts: none -> 6.01 us  [shards(): jnp.stack([both] * lax.axis_size('dp'))]
  transfers between devices with their start and end apart: 12 -> 12, of which waited for: 5 -> 5; matrix products, arithmetic and copies ran while one was open for 19% -> 8% of each run, Pallas kernels for 0% -> 0%
where the time goes in v1:
time: 551 us; the launch traced here: 543 us
  waiting for transfers between devices  422 us (77%)
  starting transfers between devices  49.7 us (9%)
  matrix products  33.6 us (6%)
  local copies, waits for them, and re-layouts  18.6 us (3%)
  other arithmetic  17.5 us (3%)
    all_to_all x1, waiting for transfers between devices, shards(): lax.all_to_all(jnp.stack([both] * lax.axis_size('dp')), 'dp', 0, 0)  354 us
    all_to_all x2, waiting for transfers between devices, exchange(): lax.all_to_all(filled, 'dp', split_axis=0, concat_axis=0, tiled=True)  66.4 us
    dot_general x15, matrix products, mm(): return jnp.dot(a, b, preferred_element_type=F32)  32.7 us
    all_to_all x2, starting transfers between devices, exchange(): lax.all_to_all(filled, 'dp', split_axis=0, concat_axis=0, tiled=True)  24.5 us
    ppermute x9, starting transfers between devices, swap(): return lax.ppermute(value, 'pipe', [(0, 1), (1, 0)])  17.5 us
  transfers between devices with their start and end apart: 12, of which 5 were waited for; matrix products, arithmetic and copies ran while one was open for 8% of the time, Pallas kernels for 0%

profile of v1, /device:TPU:1, one launch (start us, length us, event | category | flops | bytes accessed | tf_op | source)
XLA Modules:
  0.0 543.1 jit_solution(3244669355442367496)
XLA Ops:
  4.0 2.2 fusion.12
  6.2 16.3 %all-to-all-start.1 = ((bf16[128,8,1152]{2,1,0:T(8,128)(2,1)}), bf16[128,8,1152]{2,1,0:T(8,128)(2,1)S(1)}, u32[]{:S(2)}, u32[]{:S(2)}) async-start(bf16[128,8,1152]{2,1,0:T(8,128)(2,1)} %fusion.12), calls=%async_computation.1 | async-start | bytes 4718592 | tf_op jit(solution)/shard_map/all_to_all | solution.py:148
  25.2 55.6 %all-to-all-done.1 = bf16[128,8,1152]{2,1,0:T(8,128)(2,1)S(1)} async-done(((bf16[128,8,1152]{2,1,0:T(8,128)(2,1)}), bf16[128,8,1152]{2,1,0:T(8,128)(2,1)S(1)}, u32[]{:S(2)}, u32[]{:S(2)}) %all-to-all-start.1) | async-done | bytes 2359328 | tf_op jit(solution)/shard_map/all_to_all | solution.py:148
  80.8 6.0 %stack.2 = bf16[128,16,4096]{2,1,0:T(8,128)(2,1)} broadcast(bf16[16,4096]{1,0:T(8,128)(2,1)S(1)} %pad_maximum_fusion.20), dimensions={1,2} | broadcast | bytes 16908288 | tf_op jit(solution)/shard_map/stack | solution.py:98
  86.8 7.7 %all-to-all-start = ((bf16[128,16,4096]{2,1,0:T(8,128)(2,1)}), bf16[128,16,4096]{2,1,0:T(8,128)(2,1)}, u32[]{:S(2)}, u32[]{:S(2)}) async-start(bf16[128,16,4096]{2,1,0:T(8,128)(2,1)} %stack.2), calls=%async_computation | async-start | bytes 33554432 | tf_op jit(solution)/shard_map/all_to_all | solution.py:98
  94.6 2.8 collective-permute-start
  104.4 354.4 %all-to-all-done = bf16[128,16,4096]{2,1,0:T(8,128)(2,1)} async-done(((bf16[128,16,4096]{2,1,0:T(8,128)(2,1)}), bf16[128,16,4096]{2,1,0:T(8,128)(2,1)}, u32[]{:S(2)}, u32[]{:S(2)}) %all-to-all-start) | async-done | bytes 16777248 | tf_op jit(solution)/shard_map/all_to_all | solution.py:98
  458.8 3.9 fusion.273
  462.7 5.6 %fusion.281 = (bf16[128,1536]{0,1:T(8,128)(2,1)S(1)}, f32[128,1536]{0,1:T(8,128)S(1)}) fusion(f32[1536]{0:T(1024)S(1)} %select_n.239, bf16[2048,4096]{1,0:T(8,128)(2,1)} %bitcast.6, bf16[128,2048]{0,1:T(8,128)(2,1)S(1)} %copy-done.6, f32[2048]{0:T(1024)S(1)} %get-tuple-element.73, f32[2048]{0:T(1024)S(1)} %get-tuple-element.71, f32[128]{0:T(128)S(1)} %rsqrt.36, ...), kind=kOutput, calls=%fused_computation.381 | convolution fusion | flops 807272448 | bytes 8018944 | tf_op jit(solution)/shard_map/dot_general | solution.py:21
  470.9 8.1 %all-to-all-start.2 = ((bf16[128,8,512]{2,1,0:T(8,128)(2,1)}), bf16[128,8,512]{2,1,0:T(8,128)(2,1)}, u32[]{:S(2)}, u32[]{:S(2)}) async-start(bf16[128,8,512]{2,1,0:T(8,128)(2,1)} %fusion.40), calls=%async_computation.2 | async-start | bytes 2097152 | tf_op jit(solution)/shard_map/all_to_all | solution.py:148
  479.2 1.7 pad_maximum_fusion.17
  480.9 4.7 collective-permute-start.3
  486.5 1.6 pad_maximum_fusion.18
  488.6 5.1 fusion.288
  494.4 10.8 %all-to-all-done.2 = bf16[128,8,512]{2,1,0:T(8,128)(2,1)} async-done(((bf16[128,8,512]{2,1,0:T(8,128)(2,1)}), bf16[128,8,512]{2,1,0:T(8,128)(2,1)}, u32[]{:S(2)}, u32[]{:S(2)}) %all-to-all-start.2) | async-done | bytes 1048608 | tf_op jit(solution)/shard_map/all_to_all | solution.py:148
  505.2 1.5 convolution_convert_fusion.3
  506.8 6.5 %collective-permute-start.7 = (bf16[128,512]{1,0:T(8,128)(2,1)S(1)}, bf16[128,512]{1,0:T(8,128)(2,1)S(1)}, u32[]{:S(2)}, u32[]{:S(2)}) collective-permute-start(bf16[128,512]{1,0:T(8,128)(2,1)S(1)} %convolution_convert_fusion.3), channel_id=1, source_target_pairs={{0,128},{128,0},{1,129},{129,1},{2,130},{130,2},{3,131},{131,3},{4... | collective-permute-start | bytes 393224 | tf_op jit(solution)/shard_map/ppermute | solution.py:17
  513.3 3.0 broadcast_select_fusion.3
  516.3 1.8 convert_reduce_fusion.1
  518.4 5.6 %fusion.284 = (bf16[128,1536]{0,1:T(8,128)(2,1)S(1)}, f32[128,1536]{0,1:T(8,128)S(1)}) fusion(f32[1536]{0:T(1024)S(1)} %select_n.250, bf16[2048,4096]{1,0:T(8,128)(2,1)} %bitcast.6, bf16[128,2048]{0,1:T(8,128)(2,1)S(1)} %get-tuple-element.95, f32[2048]{0:T(1024)S(1)} %copy-done.20, f32[2048]{0:T(1024)S(1)} %copy-done.19, f32[128]{0:T(128)S(1)} %add_rsqrt_fusion.3, ...), kind=kOutput, calls=%fused_computation.384 | convolution fusion | flops 807272448 | bytes 8018944 | tf_op jit(solution)/shard_map/dot_general | solution.py:21
  525.6 2.6 broadcast_select_fusion.1
  528.3 1.8 fusion.287
  530.4 4.2 fusion.289
  539.0 1.7 fusion.37
  (179 shorter events, 26.1 us)
Async XLA Ops:
  2.0 20.6 %copy-start.11 = (bf16[1,16,3072]{2,1,0:T(8,128)(2,1)S(1)}, bf16[1,16,3072]{2,1,0:T(8,128)(2,1)}, u32[]{:S(2)}) copy-start(bf16[1,16,3072]{2,1,0:T(8,128)(2,1)} %param.14) | copy-start | bytes 294916
  2.9 466.1 %copy-start.28 = (s32[128]{0:T(128)}, s32[128]{0:T(128)S(1)}, u32[]{:S(2)}) copy-start(s32[128]{0:T(128)S(1)} %get-tuple-element.110) | copy-start | bytes 1540
  3.7 465.3 %copy-start.26 = (s32[128]{0:T(128)}, s32[128]{0:T(128)S(1)}, u32[]{:S(2)}) copy-start(s32[128]{0:T(128)S(1)} %eq.107) | copy-start | bytes 1540
  3.8 464.5 %copy-start.32 = (f32[128]{0:T(128)}, f32[128]{0:T(128)S(1)}, u32[]{:S(2)}) copy-start(f32[128]{0:T(128)S(1)} %get-tuple-element.12) | copy-start | bytes 1540
  3.8 18.8 %copy-start.34 = (s32[128]{0:T(128)}, s32[128]{0:T(128)S(1)}, u32[]{:S(2)}) copy-start(s32[128]{0:T(128)S(1)} %add_add_fusion) | copy-start | bytes 1540
  3.9 19.3 %copy-start.16 = (bf16[1,8,2048]{2,1,0:T(8,128)(2,1)S(1)}, bf16[1,8,2048]{2,1,0:T(8,128)(2,1)}, u32[]{:S(2)}) copy-start(bf16[1,8,2048]{2,1,0:T(8,128)(2,1)} %param.16) | copy-start | bytes 98308
  6.2 74.6 %all-to-all-start.1 = ((bf16[128,8,1152]{2,1,0:T(8,128)(2,1)}), bf16[128,8,1152]{2,1,0:T(8,128)(2,1)S(1)}, u32[]{:S(2)}, u32[]{:S(2)}) async-start(bf16[128,8,1152]{2,1,0:T(8,128)(2,1)} %fusion.12), calls=%async_computation.1 | async-start | bytes 4718592 | tf_op jit(solution)/shard_map/all_to_all | solution.py:148
  23.2 1.9 collective-permute-start.1
  86.8 10.6 %copy-start.2 = (bf16[4,32,2048]{2,1,0:T(8,128)(2,1)S(1)}, bf16[4,32,2048]{2,1,0:T(8,128)(2,1)}, u32[]{:S(2)}) copy-start(bf16[4,32,2048]{2,1,0:T(8,128)(2,1)} %param.9) | copy-start | bytes 1572868
  86.8 371.9 %all-to-all-start = ((bf16[128,16,4096]{2,1,0:T(8,128)(2,1)}), bf16[128,16,4096]{2,1,0:T(8,128)(2,1)}, u32[]{:S(2)}, u32[]{:S(2)}) async-start(bf16[128,16,4096]{2,1,0:T(8,128)(2,1)} %stack.2), calls=%async_computation | async-start | bytes 33554432 | tf_op jit(solution)/shard_map/all_to_all | solution.py:98
  94.6 3.7 collective-permute-start
  99.0 363.7 %copy-start.21 = (f32[2048]{0:T(1024)}, f32[2048]{0:T(1024)S(1)}, u32[]{:S(2)}) copy-start(f32[2048]{0:T(1024)S(1)} %get-tuple-element.71) | copy-start | bytes 24580
  99.0 363.7 %copy-start.23 = (f32[2048]{0:T(1024)}, f32[2048]{0:T(1024)S(1)}, u32[]{:S(2)}) copy-start(f32[2048]{0:T(1024)S(1)} %get-tuple-element.73) | copy-start | bytes 24580
  100.3 3.3 collective-permute-start.6
  470.9 34.3 %all-to-all-start.2 = ((bf16[128,8,512]{2,1,0:T(8,128)(2,1)}), bf16[128,8,512]{2,1,0:T(8,128)(2,1)}, u32[]{:S(2)}, u32[]{:S(2)}) async-start(bf16[128,8,512]{2,1,0:T(8,128)(2,1)} %fusion.40), calls=%async_computation.2 | async-start | bytes 2097152 | tf_op jit(solution)/shard_map/all_to_all | solution.py:148
  480.9 32.4 %collective-permute-start.3 = (bf16[1024,1024]{1,0:T(8,128)(2,1)}, bf16[1024,1024]{1,0:T(8,128)(2,1)}, u32[]{:S(2)}, u32[]{:S(2)}) collective-permute-start(bf16[1024,1024]{1,0:T(8,128)(2,1)} %pad_maximum_fusion.17), channel_id=1, source_target_pairs={{0,128},{128,0},{1,129},{129,1},{2,130},{130,2},{3,131},{131,3},{4... | collective-permute-start | bytes 6291464 | tf_op jit(solution)/shard_map/ppermute | solution.py:17
  486.2 7.5 %collective-permute-start.2 = (bf16[128,512]{1,0:T(8,128)(2,1)S(1)}, bf16[128,512]{1,0:T(8,128)(2,1)S(1)}, u32[]{:S(2)}, u32[]{:S(2)}) collective-permute-start(bf16[128,512]{1,0:T(8,128)(2,1)S(1)} %pad_maximum_fusion.21), channel_id=1, source_target_pairs={{0,128},{128,0},{1,129},{129,1},{2,130},{130,2},{3,131},{131,3},{4... | collective-permute-start | bytes 393224 | tf_op jit(solution)/shard_map/ppermute | solution.py:17
  488.1 37.4 %collective-permute-start.5 = (bf16[1024,1024]{1,0:T(8,128)(2,1)}, bf16[1024,1024]{1,0:T(8,128)(2,1)}, u32[]{:S(2)}, u32[]{:S(2)}) collective-permute-start(bf16[1024,1024]{1,0:T(8,128)(2,1)} %pad_maximum_fusion.18), channel_id=1, source_target_pairs={{0,128},{128,0},{1,129},{129,1},{2,130},{130,2},{3,131},{131,3},{4... | collective-permute-start | bytes 6291464 | tf_op jit(solution)/shard_map/ppermute | solution.py:17
  506.7 9.5 %copy-start.7 = (bf16[128,2048]{0,1:T(8,128)(2,1)S(1)}, bf16[128,2048]{0,1:T(8,128)(2,1)}, u32[]{:S(2)}) copy-start(bf16[128,2048]{0,1:T(8,128)(2,1)} %copy-done.5) | copy-start | bytes 1572868
  506.7 9.5 %copy-start.9 = (bf16[128,512]{1,0:T(8,128)(2,1)S(1)}, bf16[128,512]{1,0:T(8,128)(2,1)}, u32[]{:S(2)}) copy-start(bf16[128,512]{1,0:T(8,128)(2,1)} %get-tuple-element.62) | copy-start | bytes 393220
  506.8 9.5 %copy-start.10 = (bf16[128,512]{1,0:T(8,128)(2,1)S(1)}, bf16[128,512]{1,0:T(8,128)(2,1)}, u32[]{:S(2)}) copy-start(bf16[128,512]{1,0:T(8,128)(2,1)} %get-tuple-element.63) | copy-start | bytes 393220
  506.8 21.4 %collective-permute-start.7 = (bf16[128,512]{1,0:T(8,128)(2,1)S(1)}, bf16[128,512]{1,0:T(8,128)(2,1)S(1)}, u32[]{:S(2)}, u32[]{:S(2)}) collective-permute-start(bf16[128,512]{1,0:T(8,128)(2,1)S(1)} %convolution_convert_fusion.3), channel_id=1, source_target_pairs={{0,128},{128,0},{1,129},{129,1},{2,130},{130,2},{3,131},{131,3},{4... | collective-permute-start | bytes 393224 | tf_op jit(solution)/shard_map/ppermute | solution.py:17
  525.2 13.6 %collective-permute-start.4 = (bf16[128,512]{1,0:T(8,128)(2,1)S(1)}, bf16[128,512]{1,0:T(8,128)(2,1)S(1)}, u32[]{:S(2)}, u32[]{:S(2)}) collective-permute-start(bf16[128,512]{1,0:T(8,128)(2,1)S(1)} %pad_maximum_fusion.22), channel_id=1, source_target_pairs={{0,128},{128,0},{1,129},{129,1},{2,130},{130,2},{3,131},{131,3},{4... | collective-permute-start | bytes 393224 | tf_op jit(solution)/shard_map/ppermute | solution.py:17
  538.3 3.4 collective-permute-start.8
  (24 other events, 129.6 us)
